TPU v7x, 32 devices: a whole 2x2x4 slice. The times are simulated.
32 devices in a mesh: groups: 2 (over y), tiles: 4 (over z), heads: 2 (over x), kv: 2 (over core).
Axes of the slice: x: 2, y: 2, z: 4, core: 2. Of those that a mesh axis runs over, the one named last changes fastest.
Arguments:
- features: bfloat16 [12288, 1536], P(('groups', 'tiles')), parts along dimension 0, may hold values from -6 to 6
- counts: int32 [8], P(('groups', 'tiles')), parts along dimension 0, may hold values from 1 to 6
- tile_mask: int32 [48, 256], P(('groups', 'tiles')), parts along dimension 0, may hold values from 0 to 1, as said below
- queries: bfloat16 [256, 768], P(('heads', 'kv')), may hold values from -6 to 6
- norm_gain: float32 [2, 768], replicated, may hold values from 0.5 to 1.5
- head_scale: float32 [12], P('heads'), may hold values from 1 to 4
- w_query: bfloat16 [2, 768, 768], P(None, None, ('heads', 'kv')), may hold values from -0.21875 to 0.21875
- w_kv: bfloat16 [2, 1536, 2, 768], P(None, None, 'kv', 'heads'), may hold values from -0.15625 to 0.15625
- w_out: bfloat16 [2, 768, 768], P(None, ('heads', 'kv')), may hold values from -0.21875 to 0.21875
Outputs:
- query_states: float32 [512, 768], P(('groups', 'heads', 'kv')), parts along dimension 0
There are 2 independent parts, one for each index of `groups`. A program takes and returns all parts, laid end to end along the dimension named above; an argument that names none is the same for every part. Nothing has to cross between parts.
Inputs may be any that keep to these rules, and one draw needn't show every extreme that they name: `tile_mask`: the first tile of every block slot is 1.
All inputs are finite; a program needn't handle non-finite values.
Results may differ from a plain program's by a relative error of at most 0.012.
The roundings to bfloat16 on the way count: a program that leaves them out, or rounds other values in their place, can miss the bound.
Values may be sent and summed in bfloat16 or wider, within the bound.
A program may use at most 64 MiB of HBM per device.

v0:
```python
import math

import jax
import jax.numpy as jnp
from jax import lax
from jax.sharding import PartitionSpec as P

SOFT_CAP = 50.0
NORM_EPS = 1e-06


def normalize(hidden, gain_row):
    return (
        hidden * lax.rsqrt(jnp.mean(hidden * hidden, axis=-1, keepdims=True) + NORM_EPS) * gain_row
    )


def body(features, counts, tile_mask, queries, norm_gain, head_scale, w_query, w_kv, w_out):
    slot_count = tile_mask.shape[0]
    block_rows = tile_mask.shape[1]
    total_rows = slot_count * block_rows
    half_rows = total_rows // 2
    layer_count = w_kv.shape[0]
    head_cols = w_kv.shape[3]
    heads_local = head_scale.shape[0]
    head_dim = head_cols // heads_local
    kv_side = lax.axis_index("kv")
    kv_weights = w_kv[:, :, 0, :]
    slot_ids = jnp.arange(slot_count, dtype=jnp.int32)

    def add_block(slot_at, current):
        block_feats = lax.dynamic_slice_in_dim(features, slot_at * block_rows, block_rows, 0)
        result = jnp.einsum(
            "rf,lfc->lrc", block_feats, kv_weights, preferred_element_type=jnp.float32
        )
        return lax.dynamic_update_slice_in_dim(
            current, result.astype(jnp.bfloat16), slot_at * block_rows, 1
        )

    own_count = counts[0]
    projected = jnp.zeros((layer_count, total_rows, head_cols), jnp.bfloat16)
    projected = lax.fori_loop(jnp.int32(0), own_count, add_block, projected)
    live_mask = tile_mask * (slot_ids < own_count).astype(jnp.int32)[:, None]
    kv_local = lax.all_to_all(projected, "kv", split_axis=1, concat_axis=2, tiled=True)
    valid_tiles = lax.dynamic_slice_in_dim(
        live_mask.reshape(total_rows).astype(jnp.float32), kv_side * half_rows, half_rows, 0
    )
    states = queries.astype(jnp.float32)
    scale_vec = head_scale / math.sqrt(head_dim)
    for layer_at in range(layer_count):
        normed = lax.all_gather(
            normalize(states, norm_gain[layer_at]).astype(jnp.bfloat16),
            ("heads", "kv"),
            axis=0,
            tiled=True,
        )
        query_part = jnp.dot(normed, w_query[layer_at], preferred_element_type=jnp.float32).astype(
            jnp.bfloat16
        )
        query_cols = lax.all_gather(query_part, "kv", axis=1, tiled=True)
        n_queries = query_cols.shape[0]
        query_heads = query_cols.reshape(n_queries, heads_local, head_dim)
        key_heads = kv_local[layer_at, :, :head_cols].reshape(half_rows, heads_local, head_dim)
        value_heads = kv_local[layer_at, :, head_cols:].reshape(half_rows, heads_local, head_dim)
        scores = jnp.einsum(
            "qhd,khd->hqk", query_heads, key_heads, preferred_element_type=jnp.float32
        )
        scores = scores * scale_vec[:, None, None]
        capped = SOFT_CAP * jnp.tanh(scores / SOFT_CAP)
        weights_p = jnp.exp(capped) * valid_tiles[None, None, :]
        totals = jnp.sum(weights_p, axis=2)
        partial_value = jnp.einsum(
            "hqk,khd->qhd",
            weights_p.astype(jnp.bfloat16),
            value_heads,
            preferred_element_type=jnp.float32,
        )
        totals, partial_value = lax.psum((totals, partial_value), ("tiles", "kv"))
        attended = (
            (partial_value / jnp.transpose(totals)[:, :, None])
            .reshape(n_queries, head_cols)
            .astype(jnp.bfloat16)
        )
        own_cols = lax.dynamic_slice_in_dim(attended, kv_side * (head_cols // 2), head_cols // 2, 1)
        states = states + lax.psum_scatter(
            jnp.dot(own_cols, w_out[layer_at], preferred_element_type=jnp.float32),
            ("heads", "kv"),
            scatter_dimension=0,
            tiled=True,
        )
    return states


def solution(mesh):
    return jax.shard_map(
        body,
        mesh=mesh,
        in_specs=(
            P(("groups", "tiles"), None),
            P(("groups", "tiles")),
            P(("groups", "tiles"), None),
            P(("heads", "kv"), None),
            P(),
            P("heads"),
            P(None, None, ("heads", "kv")),
            P(None, None, "kv", "heads"),
            P(None, ("heads", "kv"), None),
        ),
        out_specs=P(("groups", "heads", "kv"), None),
        check_vma=False,
    )
```

profile of v0, /device:TPU:0, one launch (start us, length us, event | category | flops | bytes accessed | tf_op | source)
XLA Modules:
  0.0 246.1 jit_solution(7759159386574023676)
XLA Ops:
  6.5 1.3 broadcast_in_dim.2.clone
  7.8 8.4 %while.10 = (s32[]{:T(128)}, bf16[2,1536,384]{2,0,1:T(2,128)(2,1)S(1)}, s32[]{:T(128)}, bf16[1536,1536]{1,0:T(8,128)(2,1)}, bf16[2,1536,384]{2,1,0:T(8,128)(2,1)...) while((s32[]{:T(128)}, bf16[2,1536,384]{2,0,1:T(2,128)(2,1)S(1)}, s32[]{:T(128)}, ...), condition=%wide.region_1.0_spmd, body=%wide.region_0.0_spmd.sunk | while | flops 604176384 | bytes 4325523 | solution.py:42
  8.5 2.7 %fusion.55 = bf16[2,256,384]{2,1,0:T(8,128)(2,1)S(1)} fusion(bf16[2,1536,384]{2,1,0:T(8,128)(2,1)} %get-tuple-element.108, bf16[1536,1536]{1,0:T(8,128)(2,1)} %get-tuple-element.107, s32[]{:T(128)S(6)} %select_n.14), kind=kOutput, calls=%fused_computation.1.clone.1 | convolution fusion | flops 604176384 | bytes 3538948 | tf_op jit(solution)/shard_map/while/body/rf,lfc->lrc/dot_general | solution.py:33
  11.2 0.5 copy_dynamic-update-slice_fusion.2
  12.3 2.7 %fusion.55 = bf16[2,256,384]{2,1,0:T(8,128)(2,1)S(1)} fusion(bf16[2,1536,384]{2,1,0:T(8,128)(2,1)} %get-tuple-element.108, bf16[1536,1536]{1,0:T(8,128)(2,1)} %get-tuple-element.107, s32[]{:T(128)S(6)} %select_n.14), kind=kOutput, calls=%fused_computation.1.clone.1 | convolution fusion | flops 604176384 | bytes 3538948 | tf_op jit(solution)/shard_map/while/body/rf,lfc->lrc/dot_general | solution.py:33
  15.0 0.5 copy_dynamic-update-slice_fusion.2
  16.2 1.4 copy-done
  17.6 4.0 %all-to-all-start = ((bf16[2,1536,384]{2,0,1:T(2,128)(2,1)}), bf16[2,1536,384]{2,0,1:T(2,128)(2,1)S(1)}, u32[]{:S(2)}, u32[]{:S(2)}) async-start(bf16[2,1536,384]{2,0,1:T(2,128)(2,1)} %copy-done), calls=%async_computation | async-start | bytes 4718592 | tf_op jit(solution)/shard_map/all_to_all | solution.py:44
  22.7 7.9 %all_gather.12 = bf16[256,768]{1,0:T(8,128)(2,1)S(1)} all-gather(bf16[64,768]{1,0:T(8,128)(2,1)S(1)} %fusion.30), channel_id=1, replica_groups=mesh['groups'=2,'tiles'=4,'heads'=2,'kv'=2] {'heads','kv'}, dimensions={0}, use_global_device_ids=true | all-gather | bytes 491520 | tf_op jit(solution)/shard_map/all_gather | solution.py:51
  30.6 1.3 convolution_convert_fusion.2
  31.9 1.9 all_gather.13
  33.8 5.5 %copy.12 = bf16[2,768,2,384]{1,3,2,0:T(8,128)(2,1)} copy(bf16[2,768,2,384]{3,0,1,2:T(2,128)(2,1)S(1)} %bitcast.53) | data formatting | bytes 4718592 | tf_op jit(solution)/shard_map/all_to_all | solution.py:44
  39.3 1.8 fusion.40
  41.1 1.8 fusion.4
  43.0 2.2 fusion.12
  45.3 33.3 %psum.29 = f32[256,6]{0,1:T(8,128)S(1)} all-reduce(f32[256,6]{0,1:T(8,128)S(1)} %bitcast.63), channel_id=1, replica_groups=mesh['groups'=2,'tiles'=4,'heads'=2,'kv'=2] {'tiles','kv'}, use_global_device_ids=true, to_apply=%region_5.0 | all-reduce | flops 1536 | bytes 12288 | tf_op jit(solution)/shard_map/psum | solution.py:78
  78.6 38.7 %all-reduce.3.cloned.1.call-done = f32[256,6,64]{0,2,1:T(8,128)} async-done(((f32[256,6,64]{0,2,1:T(8,128)}), f32[256,6,64]{0,2,1:T(8,128)}) %all-reduce.3.cloned.1.call-update) | async-done | bytes 393232 | tf_op jit(solution)/shard_map/psum | solution.py:78
  117.4 1.0 divide_convert_fusion.1
  118.4 1.2 fusion.21
  119.7 22.5 %reduce-scatter.3.cloned.1.call-done = f32[64,768]{1,0:T(8,128)} async-done(((f32[256,768]{1,0:T(8,128)}), f32[64,768]{1,0:T(8,128)}) %reduce-scatter.3.cloned.1.call-update) | async-done | bytes 196624 | tf_op jit(solution)/shard_map/reduce_scatter | solution.py:85
  142.2 1.1 multiply_reduce_fusion
  143.3 1.0 multiply_convert_fusion
  144.3 6.1 %all_gather.14 = bf16[256,768]{1,0:T(8,128)(2,1)S(1)} all-gather(bf16[64,768]{1,0:T(8,128)(2,1)S(1)} %multiply_convert_fusion), channel_id=1, replica_groups=mesh['groups'=2,'tiles'=4,'heads'=2,'kv'=2] {'heads','kv'}, dimensions={0}, use_global_device_ids=true | all-gather | bytes 491520 | tf_op jit(solution)/shard_map/all_gather | solution.py:51
  150.7 1.9 all_gather.15
  152.7 1.8 fusion.6
  154.5 2.2 fusion.15
  156.8 17.2 %psum.31 = f32[256,6]{0,1:T(8,128)S(1)} all-reduce(f32[256,6]{0,1:T(8,128)S(1)} %bitcast.64), channel_id=1, replica_groups=mesh['groups'=2,'tiles'=4,'heads'=2,'kv'=2] {'tiles','kv'}, use_global_device_ids=true, to_apply=%region_10.0 | all-reduce | flops 1536 | bytes 12288 | tf_op jit(solution)/shard_map/psum | solution.py:78
  174.1 39.2 %all-reduce.5.cloned.1.call-done = f32[256,6,64]{0,2,1:T(8,128)} async-done(((f32[256,6,64]{0,2,1:T(8,128)}), f32[256,6,64]{0,2,1:T(8,128)}) %all-reduce.5.cloned.1.call-update) | async-done | bytes 393232 | tf_op jit(solution)/shard_map/psum | solution.py:78
  213.3 1.0 divide_convert_fusion
  214.3 1.2 fusion.18
  215.5 22.4 %reduce-scatter.5.cloned.1.call-done = f32[64,768]{1,0:T(8,128)} async-done(((f32[256,768]{1,0:T(8,128)}), f32[64,768]{1,0:T(8,128)}) %reduce-scatter.5.cloned.1.call-update) | async-done | bytes 196624 | tf_op jit(solution)/shard_map/reduce_scatter | solution.py:85
  237.9 1.6 fusion.33
  (35 shorter events, 1.0 us)
Async XLA Ops:
  16.2 1.4 copy-start
  17.6 4.7 %copy-start.7 = (f32[6]{0:T(128)S(1)}, f32[6]{0:T(128)}, u32[]{:S(2)}) copy-start(f32[6]{0:T(128)} %param.16) | copy-start | bytes 76
  17.6 4.7 %copy-start.1 = (bf16[64,768]{1,0:T(8,128)(2,1)S(1)}, bf16[64,768]{1,0:T(8,128)(2,1)}, u32[]{:S(2)}) copy-start(bf16[64,768]{1,0:T(8,128)(2,1)} %param.14) | copy-start | bytes 294916
  17.6 4.8 %copy-start.4 = (s32[6,256]{1,0:T(8,128)S(1)}, s32[6,256]{1,0:T(8,128)}, u32[]{:S(2)}) copy-start(s32[6,256]{1,0:T(8,128)} %param.13) | copy-start | bytes 18436
  17.6 4.9 %copy-start.5 = (f32[2,768]{1,0:T(2,128)S(1)}, f32[2,768]{1,0:T(2,128)}, u32[]{:S(2)}) copy-start(f32[2,768]{1,0:T(2,128)} %param.15) | copy-start | bytes 18436
  17.6 16.2 %all-to-all-start = ((bf16[2,1536,384]{2,0,1:T(2,128)(2,1)}), bf16[2,1536,384]{2,0,1:T(2,128)(2,1)S(1)}, u32[]{:S(2)}, u32[]{:S(2)}) async-start(bf16[2,1536,384]{2,0,1:T(2,128)(2,1)} %copy-done), calls=%async_computation | async-start | bytes 4718592 | tf_op jit(solution)/shard_map/all_to_all | solution.py:44
  21.6 95.8 %all-reduce.3.cloned.1.call-start = ((), (), s32[]{:S(2)}) async-start(), calls=%async_computation.3 | async-start | bytes 786432 | tf_op jit(solution)/shard_map/psum | solution.py:78
  43.0 75.4 %copy-start.3 = (bf16[2,192,768]{2,1,0:T(8,128)(2,1)S(1)}, bf16[2,192,768]{2,1,0:T(8,128)(2,1)}, u32[]{:S(2)}) copy-start(bf16[2,192,768]{2,1,0:T(8,128)(2,1)} %param.19) | copy-start | bytes 1769476
  43.0 107.5 %copy-start.6 = (bf16[2,768,192]{1,2,0:T(8,128)(2,1)S(1)}, bf16[2,768,192]{1,2,0:T(8,128)(2,1)}, u32[]{:S(2)}) copy-start(bf16[2,768,192]{1,2,0:T(8,128)(2,1)} %param.17) | copy-start | bytes 1769476
  45.2 96.9 %reduce-scatter.3.cloned.1.call-start = ((), (), s32[]{:S(2)}) async-start(), calls=%async_computation.4 | async-start | bytes 983040 | tf_op jit(solution)/shard_map/reduce_scatter | solution.py:85
  119.6 93.6 %all-reduce.5.cloned.1.call-start = ((), (), s32[]{:S(2)}) async-start(), calls=%async_computation.5 | async-start | bytes 786432 | tf_op jit(solution)/shard_map/psum | solution.py:78
  154.5 83.4 %copy-start.2 = (f32[64,768]{1,0:T(8,128)S(1)}, f32[64,768]{1,0:T(8,128)}, u32[]{:S(2)}) copy-start(f32[64,768]{1,0:T(8,128)} %reduce-scatter.3.cloned.1.call-done) | copy-start | bytes 589828
  156.8 81.1 %reduce-scatter.5.cloned.1.call-start = ((), (), s32[]{:S(2)}) async-start(), calls=%async_computation.6 | async-start | bytes 983040 | tf_op jit(solution)/shard_map/reduce_scatter | solution.py:85
Sparse Core Ops, SparseCore 0:
  45.4 71.9 all-reduce.2
  119.9 22.2 reduce-scatter.2
  156.9 56.2 all-reduce.4
  215.6 22.2 reduce-scatter.4
where the time goes:
time: 247 us; the launch traced here: 246 us
  waiting for transfers between devices  123 us (50%)
  blocking collectives  68.5 us (28%)
  matrix products  17.5 us (7%)
  between operations  14 us (6%)
  local copies, waits for them, and re-layouts  11 us (4%)
  other arithmetic  6.06 us (2%)
  starting transfers between devices  4.12 us (2%)
    psum x2, waiting for transfers between devices, body(): totals, partial_value = lax.psum((totals, partial_value), ('tiles', 'kv'))  77.9 us
    psum x2, blocking collectives, body(): totals, partial_value = lax.psum((totals, partial_value), ('tiles', 'kv'))  50.6 us
    reduce_scatter x2, waiting for transfers between devices, body(): lax.psum_scatter(jnp.dot(own_cols, w_out[layer_at], preferred_element_typ...  44.9 us
    all_gather x2, blocking collectives, body(): lax.all_gather(normalize(states, norm_gain[layer_at]).astype(jnp.bfloat16...  14.1 us
    all_to_all x1, local copies, waits for them, and re-layouts, body(): lax.all_to_all(projected, 'kv', split_axis=1, concat_axis=2, tiled=True)  5.47 us
    dot_general x2, matrix products, add_block(): jnp.einsum('rf,lfc->lrc', block_feats, kv_weights, preferred_element_type...  5.39 us
  transfers between devices with their start and end apart: 5, of which 4 were waited for; matrix products, arithmetic and copies ran while one was open for 1% of the time, Pallas kernels for 0%

commit v1 on v0

--- a/solution.py
+++ b/solution.py
@@ -1,8 +1,11 @@
+import functools
 import math
 
 import jax
 import jax.numpy as jnp
 from jax import lax
+from jax.experimental import pallas as pl
+from jax.experimental.pallas import tpu as pltpu
 from jax.sharding import PartitionSpec as P
 
 SOFT_CAP = 50.0
@@ -91,9 +94,524 @@
     return states
 
 
+MESH = pl.DeviceIdType.MESH
+
+
+def fused_kernel(
+    n_tiles,
+    n_heads,
+    n_kv,
+    counts_ref,
+    scale_ref,
+    mask_ref,
+    gain_ref,
+    features,
+    queries,
+    w_query,
+    w_kv,
+    w_out,
+    out_ref,
+    feat_buf,
+    kvw_buf,
+    wq_buf,
+    wout_buf,
+    q_buf,
+    kv_buf,
+    kv_out,
+    valid_buf,
+    query_buf,
+    acc_buf,
+    tot_buf,
+    part_buf,
+    rs_buf,
+    att_buf,
+    attz_buf,
+    fin_buf,
+    load_sem,
+    feat_sem,
+    own_sem,
+    share_send,
+    share_recv,
+    relay_send,
+    relay_recv,
+    kv_send,
+    kv_recv,
+    rs_send,
+    rs_recv,
+    att_send,
+    att_recv,
+    qry_send,
+    qry_recv,
+    attz_send,
+    attz_recv,
+    fin_send,
+    fin_recv,
+):
+    tile_at = lax.axis_index("tiles")
+    head_at = lax.axis_index("heads")
+    kv_at = lax.axis_index("kv")
+    members = n_heads * n_kv
+    member = head_at * n_kv + kv_at
+    slots, block, _ = feat_buf.shape
+    layers = wq_buf.shape[0]
+    cols = wq_buf.shape[2]
+    width = rs_buf.shape[3]
+    own_heads = acc_buf.shape[0]
+    head_dim = acc_buf.shape[2]
+    n_queries, dq = q_buf.shape
+    tile_rows = n_queries // n_tiles
+    own_rows = n_queries // members
+    side_cols = w_kv.shape[2]
+
+    def tile_peer(step):
+        return {"tiles": lax.rem(tile_at + step, n_tiles)}
+
+    def member_peer(step):
+        other = lax.rem(member + step, members)
+        return {"heads": other // n_kv, "kv": lax.rem(other, n_kv)}
+
+    def remote(src, dst, send, recv, where):
+        return pltpu.make_async_remote_copy(
+            src_ref=src,
+            dst_ref=dst,
+            send_sem=send,
+            recv_sem=recv,
+            device_id=where,
+            device_id_type=MESH,
+        )
+
+    barrier = pltpu.get_barrier_semaphore()
+    for step in range(1, n_tiles):
+        pl.semaphore_signal(barrier, inc=1, device_id=tile_peer(step), device_id_type=MESH)
+    for step in range(1, members):
+        pl.semaphore_signal(barrier, inc=1, device_id=member_peer(step), device_id_type=MESH)
+
+    loads = [
+        pltpu.make_async_copy(
+            w_kv.at[layer],
+            kvw_buf.at[:, pl.ds(layer * side_cols, side_cols)],
+            load_sem.at[layer],
+        )
+        for layer in range(layers)
+    ]
+    feat_loads = [
+        pltpu.make_async_copy(
+            features.at[pl.ds(slot * block, block)], feat_buf.at[slot], feat_sem.at[slot]
+        )
+        for slot in range(slots)
+    ]
+    wq_load = pltpu.make_async_copy(w_query, wq_buf, load_sem.at[layers])
+    for copy in loads[:1] + feat_loads[:1] + loads[1:] + feat_loads[1:]:
+        copy.start()
+    wq_load.start()
+    own_q = pltpu.make_async_copy(
+        queries, q_buf.at[pl.ds(member * own_rows, own_rows)], own_sem.at[0]
+    )
+    own_w = [
+        pltpu.make_async_copy(w_out.at[layer], wout_buf.at[layer, member], own_sem.at[1 + layer])
+        for layer in range(layers)
+    ]
+    own_q.start()
+    for copy in own_w:
+        copy.start()
+
+    pl.semaphore_wait(barrier, n_tiles - 1 + members - 1)
+
+    def item_at(item, owner):
+        if item == 0:
+            return q_buf.at[pl.ds(owner * own_rows, own_rows)]
+        return wout_buf.at[item - 1, owner]
+
+    sources = [queries] + [w_out.at[layer] for layer in range(layers)]
+    items = range(len(sources))
+    shares = {}
+    for item in items:
+        for hop in range(1, n_heads):
+            shares[item, hop] = remote(
+                sources[item],
+                item_at(item, member),
+                share_send.at[item, hop],
+                share_recv.at[item, hop],
+                {"heads": lax.rem(head_at + hop, n_heads)},
+            )
+            shares[item, hop].start()
+    relays = {}
+
+    def start_relay(item, hop):
+        owner = lax.rem(head_at - hop + n_heads, n_heads) * n_kv + kv_at
+        src = sources[item] if hop == 0 else item_at(item, owner)
+        relays[item, hop] = remote(
+            src,
+            item_at(item, owner),
+            relay_send.at[item, hop],
+            relay_recv.at[item, hop],
+            {"kv": lax.rem(kv_at + 1, n_kv)},
+        )
+        relays[item, hop].start()
+
+    def finish_item(item):
+        for hop in range(n_heads):
+            relays[item, hop].wait()
+
+    for item in items:
+        start_relay(item, 0)
+
+    live = lax.broadcasted_iota(jnp.int32, mask_ref.shape, 0) < counts_ref[0]
+    valid_buf[...] = jnp.where(live, mask_ref[...], 0).astype(jnp.float32)
+
+    def kv_copy(slot):
+        return remote(
+            kv_out.at[slot],
+            kv_buf.at[slot, kv_at],
+            kv_send.at[slot],
+            kv_recv.at[slot],
+            {"kv": lax.rem(kv_at + 1, n_kv)},
+        )
+
+    for copy in loads:
+        copy.wait()
+
+    def project(slot, carry):
+        pltpu.make_async_copy(
+            features.at[pl.ds(0, block)], feat_buf.at[slot], feat_sem.at[slot]
+        ).wait()
+        rows = jnp.dot(feat_buf[slot], kvw_buf[...], preferred_element_type=jnp.float32)
+        for layer in range(layers):
+            at = layer * side_cols
+            low = rows[:, at : at + cols]
+            high = rows[:, at + cols : at + 2 * cols]
+            first = kv_at == 0
+            kv_buf[slot, kv_at, layer] = jnp.where(first, low, high).astype(jnp.bfloat16)
+            kv_out[slot, layer] = jnp.where(first, high, low).astype(jnp.bfloat16)
+        kv_copy(slot).start()
+        return carry
+
+    lax.fori_loop(0, slots, project, 0)
+
+    own_q.wait()
+    for hop in range(1, n_heads):
+        shares[0, hop].wait()
+        start_relay(0, hop)
+    finish_item(0)
+    wq_load.wait()
+
+    def to_query(states, layer):
+        normed = normalize(states, gain_ref[pl.ds(layer, 1)]).astype(jnp.bfloat16)
+        return jnp.dot(normed, wq_buf[layer], preferred_element_type=jnp.float32).astype(
+            jnp.bfloat16
+        )
+
+    query_buf[0] = to_query(q_buf[...].astype(jnp.float32), 0)
+    own_w[0].wait()
+    for hop in range(1, n_heads):
+        shares[1, hop].wait()
+        start_relay(1, hop)
+
+    def attend(layer):
+        acc_buf[...] = jnp.zeros_like(acc_buf)
+        tot_buf[...] = jnp.zeros_like(tot_buf)
+        lanes = tot_buf.shape[2]
+
+        def add_block(slot, carry):
+            if layer == 0:
+                kv_copy(slot).wait_recv()
+            valid_row = valid_buf[pl.ds(slot, 1)]
+            for at in range(own_heads):
+                low, high = at * head_dim, (at + 1) * head_dim
+                scale = scale_ref[kv_at * own_heads + at] * (
+                    1.0 / (math.sqrt(head_dim) * SOFT_CAP)
+                )
+                scores = lax.dot_general(
+                    query_buf[layer, :, low:high],
+                    kv_buf[slot, 0, layer, :, low:high],
+                    (((1,), (1,)), ((), ())),
+                    preferred_element_type=jnp.float32,
+                )
+                weights = jnp.exp(SOFT_CAP * jnp.tanh(scores * scale)) * valid_row
+                total = weights[:, :lanes]
+                for part in range(1, block // lanes):
+                    total = total + weights[:, part * lanes : (part + 1) * lanes]
+                tot_buf[at] += total
+                acc_buf[at] += jnp.dot(
+                    weights.astype(jnp.bfloat16),
+                    kv_buf[slot, 1, layer, :, low:high],
+                    preferred_element_type=jnp.float32,
+                )
+            return carry
+
+        lax.fori_loop(0, slots, add_block, 0)
+        tail_width = width - cols
+        lane = lax.broadcasted_iota(jnp.int32, (n_queries, tail_width), 1)
+        tail = jnp.zeros((n_queries, tail_width), jnp.float32)
+        for at in range(own_heads):
+            part_buf[layer, :, at * head_dim : (at + 1) * head_dim] = acc_buf[at].astype(
+                jnp.bfloat16
+            )
+            total = jnp.sum(tot_buf[at], axis=1, keepdims=True)
+            coarse = total.astype(jnp.bfloat16).astype(jnp.float32)
+            tail = jnp.where(lane == at, coarse, tail)
+            tail = jnp.where(lane == own_heads + at, total - coarse, tail)
+        part_buf[layer, :, cols:width] = tail.astype(jnp.bfloat16)
+        copies = []
+        for step in range(1, n_tiles):
+            other = lax.rem(tile_at + step, n_tiles)
+            copies.append(
+                remote(
+                    part_buf.at[layer, pl.ds(other * tile_rows, tile_rows)],
+                    rs_buf.at[layer, tile_at],
+                    rs_send.at[layer, step],
+                    rs_recv.at[layer, step],
+                    tile_peer(step),
+                )
+            )
+            copies[-1].start()
+        return copies
+
+    def merge(layer, copies):
+        own = part_buf[layer, pl.ds(tile_at * tile_rows, tile_rows)].astype(jnp.float32)
+        for step in range(1, n_tiles):
+            copies[step - 1].wait()
+            other = lax.rem(tile_at - step + n_tiles, n_tiles)
+            own = own + rs_buf[layer, other].astype(jnp.float32)
+        pieces = []
+        for at in range(own_heads):
+            low, high = at * head_dim, (at + 1) * head_dim
+            fine = cols + own_heads + at
+            total = own[:, cols + at : cols + at + 1] + own[:, fine : fine + 1]
+            piece = (own[:, low:high] / total).astype(jnp.bfloat16)
+            attz_buf[layer, pl.ds(tile_at * tile_rows, tile_rows), low:high] = piece
+            if layer + 1 < layers:
+                att_buf[layer, member, :, low:high] = piece
+
+    def spread_tiles(layer):
+        mine = attz_buf.at[layer, pl.ds(tile_at * tile_rows, tile_rows)]
+        copies = []
+        for step in range(1, n_tiles):
+            copies.append(
+                remote(
+                    mine,
+                    mine,
+                    attz_send.at[layer, step],
+                    attz_recv.at[layer, step],
+                    tile_peer(step),
+                )
+            )
+            copies[-1].start()
+        return copies
+
+    def spread_members(layer):
+        copies = []
+        for step in range(1, members):
+            other = lax.rem(member + step, members)
+            copies.append(
+                remote(
+                    attz_buf.at[layer, pl.ds(other * own_rows, own_rows)],
+                    fin_buf.at[layer, member],
+                    fin_send.at[layer, step],
+                    fin_recv.at[layer, step],
+                    member_peer(step),
+                )
+            )
+            copies[-1].start()
+        return copies
+
+    def project_out(layer, start, own_piece):
+        total = start
+        total = total + jnp.dot(
+            own_piece, wout_buf[layer, member], preferred_element_type=jnp.float32
+        )
+        return total
+
+    base = q_buf[pl.ds(tile_at * tile_rows, tile_rows)].astype(jnp.float32)
+    final = q_buf[pl.ds(member * own_rows, own_rows)].astype(jnp.float32)
+    pending = []
+    for layer in range(layers):
+        copies = attend(layer)
+        if layer == 0:
+            finish_item(1)
+            for slot in range(slots):
+                kv_copy(slot).wait_send()
+        for hop in range(1, n_heads):
+            if layer + 1 < layers:
+                shares[2 + layer, hop].wait()
+                start_relay(2 + layer, hop)
+        if layer > 0:
+            finish_item(1 + layer)
+            own_w[layer].wait()
+        merge(layer, copies)
+        if layer + 1 < layers:
+            mine = att_buf.at[layer, member]
+            spread = []
+            for step in range(1, members):
+                spread.append(
+                    remote(
+                        mine,
+                        mine,
+                        att_send.at[layer, step],
+                        att_recv.at[layer, step],
+                        member_peer(step),
+                    )
+                )
+                spread[-1].start()
+            over_tiles = spread_tiles(layer)
+            base = base + jnp.dot(
+                att_buf[layer, member], wout_buf[layer, member], preferred_element_type=jnp.float32
+            )
+            for step in range(1, members):
+                spread[step - 1].wait()
+                other = lax.rem(member - step + members, members)
+                base = base + jnp.dot(
+                    att_buf[layer, other],
+                    wout_buf[layer, other],
+                    preferred_element_type=jnp.float32,
+                )
+            rows = pl.ds(tile_at * tile_rows, tile_rows)
+            query_buf[layer + 1, rows] = to_query(base, layer + 1)
+            gather = []
+            for step in range(1, n_tiles):
+                mine = query_buf.at[layer + 1, rows]
+                gather.append(
+                    remote(
+                        mine,
+                        mine,
+                        qry_send.at[layer, step],
+                        qry_recv.at[layer, step],
+                        tile_peer(step),
+                    )
+                )
+                gather[-1].start()
+            for copy in over_tiles:
+                copy.wait()
+            pending.append(spread_members(layer))
+            for copy in gather:
+                copy.wait()
+        else:
+            over_tiles = spread_tiles(layer)
+            for old, copies in enumerate(pending):
+                own_piece = attz_buf[old, pl.ds(member * own_rows, own_rows)]
+                final = project_out(old, final, own_piece)
+                for step in range(1, members):
+                    copies[step - 1].wait()
+                    other = lax.rem(member - step + members, members)
+                    final = final + jnp.dot(
+                        fin_buf[old, other],
+                        wout_buf[old, other],
+                        preferred_element_type=jnp.float32,
+                    )
+            for copy in over_tiles:
+                copy.wait()
+            last = spread_members(layer)
+            own_piece = attz_buf[layer, pl.ds(member * own_rows, own_rows)]
+            final = project_out(layer, final, own_piece)
+            for step in range(1, members):
+                last[step - 1].wait()
+                other = lax.rem(member - step + members, members)
+                final = final + jnp.dot(
+                    fin_buf[layer, other],
+                    wout_buf[layer, other],
+                    preferred_element_type=jnp.float32,
+                )
+            out_ref[...] = final
+
+
+def fused_body(
+    mesh, features, counts, tile_mask, queries, norm_gain, head_scale, w_query, w_kv, w_out
+):
+    n_tiles, n_heads, n_kv = (mesh.shape[name] for name in ("tiles", "heads", "kv"))
+    members = n_heads * n_kv
+    slots, block = tile_mask.shape
+    own_rows, dq = queries.shape
+    n_queries = own_rows * members
+    tile_rows = n_queries // n_tiles
+    layers, feat, _, side_cols = w_kv.shape
+    cols = w_query.shape[2]
+    own_heads = head_scale.shape[0] // n_kv
+    head_dim = cols // own_heads
+    width = -(-(cols + 2 * own_heads) // 128) * 128
+    bf16, f32 = jnp.bfloat16, jnp.float32
+    dma = pltpu.SemaphoreType.DMA
+    any_spec = pl.BlockSpec(memory_space=pl.ANY)
+    smem = pl.BlockSpec(memory_space=pltpu.SMEM)
+    vmem = pl.BlockSpec(memory_space=pltpu.VMEM)
+    return pl.pallas_call(
+        functools.partial(fused_kernel, n_tiles, n_heads, n_kv),
+        out_shape=jax.ShapeDtypeStruct((own_rows, dq), f32),
+        in_specs=[smem, smem, vmem, vmem] + [any_spec] * 5,
+        out_specs=vmem,
+        scratch_shapes=[
+            pltpu.VMEM((slots, block, feat), bf16),
+            pltpu.VMEM((feat, layers * side_cols), bf16),
+            pltpu.VMEM((layers, dq, cols), bf16),
+            pltpu.VMEM((layers, members, cols, dq), bf16),
+            pltpu.VMEM((n_queries, dq), bf16),
+            pltpu.VMEM((slots, 2, layers, block, cols), bf16),
+            pltpu.VMEM((slots, layers, block, cols), bf16),
+            pltpu.VMEM((slots, block), f32),
+            pltpu.VMEM((layers, n_queries, cols), bf16),
+            pltpu.VMEM((own_heads, n_queries, head_dim), f32),
+            pltpu.VMEM((own_heads, n_queries, 128), f32),
+            pltpu.VMEM((layers, n_queries, width), bf16),
+            pltpu.VMEM((layers, n_tiles, tile_rows, width), bf16),
+            pltpu.VMEM((layers, members, tile_rows, cols), bf16),
+            pltpu.VMEM((layers, n_queries, cols), bf16),
+            pltpu.VMEM((layers, members, own_rows, cols), bf16),
+            dma((layers + 1,)),
+            dma((slots,)),
+            dma((layers + 1,)),
+            dma((layers + 1, n_heads)),
+            dma((layers + 1, n_heads)),
+            dma((layers + 1, n_heads)),
+            dma((layers + 1, n_heads)),
+            dma((slots,)),
+            dma((slots,)),
+            dma((layers, n_tiles)),
+            dma((layers, n_tiles)),
+            dma((layers, members)),
+            dma((layers, members)),
+            dma((layers, n_tiles)),
+            dma((layers, n_tiles)),
+            dma((layers, n_tiles)),
+            dma((layers, n_tiles)),
+            dma((layers, members)),
+            dma((layers, members)),
+        ],
+        compiler_params=pltpu.CompilerParams(
+            collective_id=0, has_side_effects=True, vmem_limit_bytes=56 * 1024 * 1024
+        ),
+    )(
+        counts,
+        head_scale,
+        tile_mask,
+        norm_gain,
+        features,
+        queries,
+        w_query,
+        w_kv.reshape(layers, feat, side_cols),
+        w_out,
+    )
+
+
+def choose(mesh, *args):
+    features, counts, tile_mask, queries, norm_gain, head_scale, w_query, w_kv, w_out = args
+    n_tiles, n_heads, n_kv = (mesh.shape[name] for name in ("tiles", "heads", "kv"))
+    n_queries = queries.shape[0] * n_heads * n_kv
+    fits = (
+        n_kv == 2
+        and n_tiles > 1
+        and n_heads > 1
+        and head_scale.shape[0] % n_kv == 0
+        and n_queries % (n_tiles * 16) == 0
+        and queries.shape[0] % 16 == 0
+        and tile_mask.shape[1] % 128 == 0
+        and w_kv.shape[3] % 128 == 0
+        and w_kv.shape[3] == n_kv * w_query.shape[2]
+    )
+    return fused_body(mesh, *args) if fits else body(*args)
+
+
 def solution(mesh):
     return jax.shard_map(
-        body,
+        functools.partial(choose, mesh),
         mesh=mesh,
         in_specs=(
             P(("groups", "tiles"), None),

time: 247 us -> 60 us (0.24)
  waiting for transfers between devices: 123 us -> 0 us
  blocking collectives: 68.5 us -> 0 us
  Pallas kernels: 0 us -> 55.3 us
  matrix products: 17.5 us -> 0 us
  between operations: 14 us -> 0.66 us
  local copies, waits for them, and re-layouts: 11 us -> 3.83 us
  other arithmetic: 6.06 us -> 0 us
  starting transfers between devices: 4.12 us -> 0 us
    psum x2 -> x0, waiting for transfers between devices: 77.9 us -> none  [body(): totals, partial_value = lax.psum((totals, partial_value), ('tiles', 'kv'))]
    pallas_call x0 -> x1, Pallas kernels: none -> 55.3 us  [fused_body(): pl.pallas_call(functools.partial(fused_kernel, n_tiles, n_heads, n_kv), o...]
    psum x2 -> x0, blocking collectives: 50.6 us -> none  [body(): totals, partial_value = lax.psum((totals, partial_value), ('tiles', 'kv'))]
    reduce_scatter x2 -> x0, waiting for transfers between devices: 44.9 us -> none  [body(): lax.psum_scatter(jnp.dot(own_cols, w_out[layer_at], preferred_element_typ...]
    all_gather x4 -> x0, blocking collectives: 18 us -> none  [the longest x2 14.1 us: body(): lax.all_gather(normalize(states, norm_gain[layer_at]).astype(jnp.bfloat16...]
    dot_general x10 -> x0, matrix products: 17.5 us -> none  [the longest x2 5.39 us: add_block(): jnp.einsum('rf,lfc->lrc', block_feats, kv_weights, preferred_element_type...]
    all_to_all x1 -> x0, local copies, waits for them, and re-layouts: 5.47 us -> none  [body(): lax.all_to_all(projected, 'kv', split_axis=1, concat_axis=2, tiled=True)]
    all_to_all x1 -> x0, starting transfers between devices: 3.95 us -> none  [body(): lax.all_to_all(projected, 'kv', split_axis=1, concat_axis=2, tiled=True)]
  transfers between devices with their start and end apart: 5 -> 0, of which waited for: 4 -> 0; matrix products, arithmetic and copies ran while one was open for 1% -> 0% of each run, Pallas kernels for 0% -> 0%
where the time goes in v1:
time: 60 us; the launch traced here: 59.8 us
  Pallas kernels  55.3 us (92%)
  local copies, waits for them, and re-layouts  3.83 us (6%)
  between operations  0.66 us (1%)
    pallas_call x1, Pallas kernels, fused_body(): pl.pallas_call(functools.partial(fused_kernel, n_tiles, n_heads, n_kv), o...  55.3 us
    unnamed x2, local copies, waits for them, and re-layouts  3.83 us

profile of v1, /device:TPU:0, one launch (start us, length us, event | category | flops | bytes accessed | tf_op | source)
XLA Modules:
  0.0 59.8 jit_solution(8676752340803302430)
XLA Ops:
  0.7 2.2 %copy.10.w_query = bf16[2,768,192]{2,1,0:T(8,128)(2,1)} copy(bf16[2,768,192]{1,2,0:T(8,128)(2,1)} %param.15) | data formatting | bytes 1179648 | tf_op args[6]
  2.9 55.3 %shard_map.91 = f32[64,768]{1,0:T(8,128)} custom-call(s32[1]{0:T(128)S(6)} %copy.12.counts_ref, f32[6]{0:T(128)} %scale_ref.1, s32[6,256]{1,0:T(8,128)} %mask_ref.1, f32[2,768]{1,0:T(2,128)} %gain_ref.1, bf16[1536,1536]{1,0:T(8,128)(2,1)} %features.1, bf16[64,768]{1,0:T(8,128)(2,1)} %queries.1, bf16[2,768,192]{2,1,0:T(8,128)(2,1)} %copy.10.w_query, ...), custom_call_target="tpu_custom_call" | custom-call | tf_op jit(solution)/shard_map/pallas_call | solution.py:536
  58.2 1.6 %copy.13 = f32[64,768]{1,0:T(8,128)} copy(f32[64,768]{1,0:T(8,128)} %shard_map.91) | data formatting | bytes 393216

commit v2 on v1

--- a/solution.py
+++ b/solution.py
@@ -154,7 +154,7 @@
     member = head_at * n_kv + kv_at
     slots, block, _ = feat_buf.shape
     layers = wq_buf.shape[0]
-    cols = wq_buf.shape[2]
+    cols = wq_buf.shape[1]
     width = rs_buf.shape[3]
     own_heads = acc_buf.shape[0]
     head_dim = acc_buf.shape[2]
@@ -215,12 +215,43 @@
     for copy in own_w:
         copy.start()
 
-    pl.semaphore_wait(barrier, n_tiles - 1 + members - 1)
-
     def item_at(item, owner):
         if item == 0:
             return q_buf.at[pl.ds(owner * own_rows, own_rows)]
         return wout_buf.at[item - 1, owner]
+
+    def kv_copy(slot):
+        return remote(
+            kv_out.at[slot],
+            kv_buf.at[slot, kv_at],
+            kv_send.at[slot],
+            kv_recv.at[slot],
+            {"kv": lax.rem(kv_at + 1, n_kv)},
+        )
+
+    for copy in loads:
+        copy.wait()
+
+    def project(send, slot, carry):
+        pltpu.make_async_copy(
+            features.at[pl.ds(0, block)], feat_buf.at[slot], feat_sem.at[slot]
+        ).wait()
+        rows = jnp.dot(feat_buf[slot], kvw_buf[...], preferred_element_type=jnp.float32)
+        for layer in range(layers):
+            at = layer * side_cols
+            low = rows[:, at : at + cols]
+            high = rows[:, at + cols : at + 2 * cols]
+            first = kv_at == 0
+            kv_buf[slot, kv_at, layer] = jnp.where(first, low, high).astype(jnp.bfloat16)
+            kv_out[slot, layer] = jnp.where(first, high, low).astype(jnp.bfloat16)
+        if send:
+            kv_copy(slot).start()
+        return carry
+
+    early = slots // 3
+    middle = slots - slots // 3
+    lax.fori_loop(0, early, functools.partial(project, False), 0)
+    pl.semaphore_wait(barrier, n_tiles - 1 + members - 1)
 
     sources = [queries] + [w_out.at[layer] for layer in range(layers)]
     items = range(len(sources))
@@ -259,47 +290,25 @@
     live = lax.broadcasted_iota(jnp.int32, mask_ref.shape, 0) < counts_ref[0]
     valid_buf[...] = jnp.where(live, mask_ref[...], 0).astype(jnp.float32)
 
-    def kv_copy(slot):
-        return remote(
-            kv_out.at[slot],
-            kv_buf.at[slot, kv_at],
-            kv_send.at[slot],
-            kv_recv.at[slot],
-            {"kv": lax.rem(kv_at + 1, n_kv)},
-        )
-
-    for copy in loads:
-        copy.wait()
-
-    def project(slot, carry):
-        pltpu.make_async_copy(
-            features.at[pl.ds(0, block)], feat_buf.at[slot], feat_sem.at[slot]
-        ).wait()
-        rows = jnp.dot(feat_buf[slot], kvw_buf[...], preferred_element_type=jnp.float32)
-        for layer in range(layers):
-            at = layer * side_cols
-            low = rows[:, at : at + cols]
-            high = rows[:, at + cols : at + 2 * cols]
-            first = kv_at == 0
-            kv_buf[slot, kv_at, layer] = jnp.where(first, low, high).astype(jnp.bfloat16)
-            kv_out[slot, layer] = jnp.where(first, high, low).astype(jnp.bfloat16)
+    for slot in range(early):
         kv_copy(slot).start()
-        return carry
-
-    lax.fori_loop(0, slots, project, 0)
-
+    lax.fori_loop(early, middle, functools.partial(project, True), 0)
     own_q.wait()
     for hop in range(1, n_heads):
         shares[0, hop].wait()
         start_relay(0, hop)
+    lax.fori_loop(middle, slots, functools.partial(project, True), 0)
     finish_item(0)
     wq_load.wait()
 
     def to_query(states, layer):
         normed = normalize(states, gain_ref[pl.ds(layer, 1)]).astype(jnp.bfloat16)
-        return jnp.dot(normed, wq_buf[layer], preferred_element_type=jnp.float32).astype(
-            jnp.bfloat16
-        )
+        return lax.dot_general(
+            normed,
+            wq_buf[layer],
+            (((1,), (1,)), ((), ())),
+            preferred_element_type=jnp.float32,
+        ).astype(jnp.bfloat16)
 
     query_buf[0] = to_query(q_buf[...].astype(jnp.float32), 0)
     own_w[0].wait()
@@ -541,7 +550,7 @@
         scratch_shapes=[
             pltpu.VMEM((slots, block, feat), bf16),
             pltpu.VMEM((feat, layers * side_cols), bf16),
-            pltpu.VMEM((layers, dq, cols), bf16),
+            pltpu.VMEM((layers, cols, dq), bf16),
             pltpu.VMEM((layers, members, cols, dq), bf16),
             pltpu.VMEM((n_queries, dq), bf16),
             pltpu.VMEM((slots, 2, layers, block, cols), bf16),
@@ -585,7 +594,7 @@
         norm_gain,
         features,
         queries,
-        w_query,
+        jnp.swapaxes(w_query, 1, 2),
         w_kv.reshape(layers, feat, side_cols),
         w_out,
     )

time: 60 us -> 59.7 us (level)
  local copies, waits for them, and re-layouts: 3.83 us -> 1.62 us
  Pallas kernels: 55.3 us -> 57.2 us
    unnamed x2 -> x1, local copies, waits for them, and re-layouts: 3.83 us -> 1.62 us
    pallas_call x1, Pallas kernels: 55.3 us -> 57.2 us  [fused_body(): pl.pallas_call(functools.partial(fused_kernel, n_tiles, n_heads, n_kv), o...]
where the time goes in v2:
time: 59.7 us; the launch traced here: 59.5 us
  Pallas kernels  57.2 us (96%)
  local copies, waits for them, and re-layouts  1.62 us (3%)
  between operations  0.66 us (1%)
    pallas_call x1, Pallas kernels, fused_body(): pl.pallas_call(functools.partial(fused_kernel, n_tiles, n_heads, n_kv), o...  57.2 us
    unnamed x1, local copies, waits for them, and re-layouts  1.62 us

profile of v2, /device:TPU:0, one launch (start us, length us, event | category | flops | bytes accessed | tf_op | source)
XLA Modules:
  0.0 59.5 jit_solution(1861786593736755070)
XLA Ops:
  0.7 57.2 %shard_map.91 = f32[64,768]{1,0:T(8,128)} custom-call(s32[1]{0:T(128)S(6)} %copy.11.counts_ref, f32[6]{0:T(128)} %scale_ref.1, s32[6,256]{1,0:T(8,128)} %mask_ref.1, f32[2,768]{1,0:T(2,128)} %gain_ref.1, bf16[1536,1536]{1,0:T(8,128)(2,1)} %features.1, bf16[64,768]{1,0:T(8,128)(2,1)} %queries.1, bf16[2,192,768]{2,1,0:T(8,128)(2,1)} %bitcast.3, ...), custom_call_target="tpu_custom_call" | custom-call | tf_op jit(solution)/shard_map/pallas_call | solution.py:545
  57.9 1.6 %copy.12 = f32[64,768]{1,0:T(8,128)} copy(f32[64,768]{1,0:T(8,128)} %shard_map.91) | data formatting | bytes 393216

commit v3 on v2

--- a/solution.py
+++ b/solution.py
@@ -94,6 +94,7 @@
     return states
 
 
+LOG2_E = math.log2(math.e)
 MESH = pl.DeviceIdType.MESH
 
 
@@ -229,10 +230,7 @@
             {"kv": lax.rem(kv_at + 1, n_kv)},
         )
 
-    for copy in loads:
-        copy.wait()
-
-    def project(send, slot, carry):
+    def project(slot, carry):
         pltpu.make_async_copy(
             features.at[pl.ds(0, block)], feat_buf.at[slot], feat_sem.at[slot]
         ).wait()
@@ -244,13 +242,10 @@
             first = kv_at == 0
             kv_buf[slot, kv_at, layer] = jnp.where(first, low, high).astype(jnp.bfloat16)
             kv_out[slot, layer] = jnp.where(first, high, low).astype(jnp.bfloat16)
-        if send:
-            kv_copy(slot).start()
+        kv_copy(slot).start()
         return carry
 
-    early = slots // 3
     middle = slots - slots // 3
-    lax.fori_loop(0, early, functools.partial(project, False), 0)
     pl.semaphore_wait(barrier, n_tiles - 1 + members - 1)
 
     sources = [queries] + [w_out.at[layer] for layer in range(layers)]
@@ -290,14 +285,14 @@
     live = lax.broadcasted_iota(jnp.int32, mask_ref.shape, 0) < counts_ref[0]
     valid_buf[...] = jnp.where(live, mask_ref[...], 0).astype(jnp.float32)
 
-    for slot in range(early):
-        kv_copy(slot).start()
-    lax.fori_loop(early, middle, functools.partial(project, True), 0)
+    for copy in loads:
+        copy.wait()
+    lax.fori_loop(0, middle, project, 0, unroll=2)
     own_q.wait()
     for hop in range(1, n_heads):
         shares[0, hop].wait()
         start_relay(0, hop)
-    lax.fori_loop(middle, slots, functools.partial(project, True), 0)
+    lax.fori_loop(middle, slots, project, 0, unroll=2)
     finish_item(0)
     wq_load.wait()
 
@@ -336,7 +331,7 @@
                     (((1,), (1,)), ((), ())),
                     preferred_element_type=jnp.float32,
                 )
-                weights = jnp.exp(SOFT_CAP * jnp.tanh(scores * scale)) * valid_row
+                weights = jnp.exp2((SOFT_CAP * LOG2_E) * jnp.tanh(scores * scale)) * valid_row
                 total = weights[:, :lanes]
                 for part in range(1, block // lanes):
                     total = total + weights[:, part * lanes : (part + 1) * lanes]
@@ -348,7 +343,7 @@
                 )
             return carry
 
-        lax.fori_loop(0, slots, add_block, 0)
+        lax.fori_loop(0, slots, add_block, 0, unroll=True)
         tail_width = width - cols
         lane = lax.broadcasted_iota(jnp.int32, (n_queries, tail_width), 1)
         tail = jnp.zeros((n_queries, tail_width), jnp.float32)

time: 59.7 us -> 51.5 us (0.86)
  Pallas kernels: 57.2 us -> 49 us
    pallas_call x1, Pallas kernels: 57.2 us -> 49 us  [fused_body(): pl.pallas_call(functools.partial(fused_kernel, n_tiles, n_heads, n_kv), o...]
where the time goes in v3:
time: 51.5 us; the launch traced here: 51.3 us
  Pallas kernels  49 us (95%)
  local copies, waits for them, and re-layouts  1.62 us (3%)
  between operations  0.66 us (1%)
    pallas_call x1, Pallas kernels, fused_body(): pl.pallas_call(functools.partial(fused_kernel, n_tiles, n_heads, n_kv), o...  49 us
    unnamed x1, local copies, waits for them, and re-layouts  1.62 us

profile of v3, /device:TPU:0, one launch (start us, length us, event | category | flops | bytes accessed | tf_op | source)
XLA Modules:
  0.0 51.3 jit_solution(9887746987954347782)
XLA Ops:
  0.7 49.0 %shard_map.91 = f32[64,768]{1,0:T(8,128)} custom-call(s32[1]{0:T(128)S(6)} %copy.11.counts_ref, f32[6]{0:T(128)} %scale_ref.1, s32[6,256]{1,0:T(8,128)} %mask_ref.1, f32[2,768]{1,0:T(2,128)} %gain_ref.1, bf16[1536,1536]{1,0:T(8,128)(2,1)} %features.1, bf16[64,768]{1,0:T(8,128)(2,1)} %queries.1, bf16[2,192,768]{2,1,0:T(8,128)(2,1)} %bitcast.3, ...), custom_call_target="tpu_custom_call" | custom-call | tf_op jit(solution)/shard_map/pallas_call | solution.py:540
  49.6 1.6 %copy.12 = f32[64,768]{1,0:T(8,128)} copy(f32[64,768]{1,0:T(8,128)} %shard_map.91) | data formatting | bytes 393216
